TPU v7x, 512 devices: a whole 4x8x8 slice. The times are simulated.
512 devices in a mesh: wide: 32 (over y, x), narrow: 16 (over z, core).
Axes of the slice: x: 4, y: 8, z: 8, core: 2. Of those that a mesh axis runs over, the one named last changes fastest.
Arguments:
- blocks: float32 [32, 16, 2, 64, 4096], P('wide', 'narrow'), may hold values from -786432 to 786432
- block_coords: int32 [32, 16, 2, 3], P('wide', 'narrow'), may hold values from 0 to 63, as said below
- block_count: int32 [32, 16], P('wide', 'narrow'), may hold values from 0 to 2, as said below
- orbital_factor: float32 [4096, 128], P('narrow'), may hold values from -8 to 8
Outputs:
- aux_new: float32 [16, 1024, 128], P('narrow', 'wide')
- orbital_new: float32 [4096, 128], P('narrow')
Inputs may be any that keep to these rules, and one draw needn't show every extreme that they name: `block_coords`: entries are (auxiliary block 0 to 15, orbital block 0 to 63, orbital block 0 to 63); no triple repeats within a column. `block_count`: slot s of a device is live when s < its count; some device holds 2 live blocks in every draw.
All inputs are finite; a program needn't handle non-finite values.
Results may differ from a plain program's by a relative error of at most 0.0003.
Values sent between devices are 32-bit elements; how exact they have to be, the bound alone decides.
A program may use at most 64 MiB of HBM per device.

v0:
```python
import jax
import jax.numpy as jnp
from jax import lax
from jax.sharding import PartitionSpec as P

NP = 16384


precise_level = lax.Precision.HIGHEST


def product(left, right):
    return jnp.dot(left, right, precision=precise_level, preferred_element_type=jnp.float32)


def inverse_of(gram):
    lower = jnp.linalg.cholesky(gram)
    return jax.scipy.linalg.cho_solve((lower, True), jnp.eye(gram.shape[0], dtype=gram.dtype))


def first_mode(tensor_block, rows_i, rows_j):
    block_edge = rows_i.shape[0]
    contracted = product(tensor_block.reshape(block_edge * block_edge, block_edge), rows_j)
    contracted = contracted.reshape(block_edge, block_edge, -1)
    return (contracted, jnp.sum(contracted * rows_i[None], axis=1))


def second_mode(tensor_block, contracted, aux_rows, rows_i):
    block_edge = rows_i.shape[0]
    term_i = jnp.sum(contracted * aux_rows[:, None, :], axis=0)
    spread = product(aux_rows.T, tensor_block).reshape(-1, block_edge, block_edge)
    term_j = jnp.einsum("rij,ir->jr", spread, rows_i, precision=precise_level)
    return (term_i, term_j)


def pick_rows(matrix, index, length):
    return lax.dynamic_slice_in_dim(matrix, index * length, length, 0)


def on_device(blocks, block_coords, block_count, orbital_factor):
    block_edge = blocks.shape[3]
    slot_count = blocks.shape[2]
    factor_rank = orbital_factor.shape[1]
    full_orbital = lax.all_gather(orbital_factor, "narrow", axis=0, tiled=True)
    orbital_rows = full_orbital.shape[0]
    gram_b = product(full_orbital.T, full_orbital)
    coords = block_coords[0, 0]
    weights = (jnp.arange(slot_count, dtype=jnp.int32) < block_count[0, 0]).astype(jnp.float32)
    column_rows = NP // lax.axis_size("narrow")
    column_blocks = column_rows // block_edge
    contractions = []
    aux_terms = []
    first_rows = []
    for slot_index in range(slot_count):
        rows_i = pick_rows(full_orbital, coords[slot_index, 1], block_edge)
        rows_j = pick_rows(full_orbital, coords[slot_index, 2], block_edge)
        contracted, aux_term = first_mode(blocks[0, 0, slot_index], rows_i, rows_j)
        contractions.append(contracted)
        aux_terms.append(aux_term)
        first_rows.append(rows_i)
    aux_onehot = (jnp.arange(column_blocks, dtype=jnp.int32)[:, None] == coords[None, :, 0]).astype(
        jnp.float32
    ) * weights[None, :]
    column_sum = jnp.einsum(
        "qs,ser->qer", aux_onehot, jnp.stack(aux_terms), precision=precise_level
    )
    column_sum = column_sum.reshape(column_rows, factor_rank)
    owned_sum = lax.psum_scatter(column_sum, "wide", scatter_dimension=0, tiled=True)
    aux_owned = product(owned_sum, inverse_of(gram_b * gram_b))
    gram_a = lax.psum(product(aux_owned.T, aux_owned), ("wide", "narrow"))
    column_aux = lax.all_gather(aux_owned, "wide", axis=0, tiled=True)
    aux_blocks = [
        pick_rows(column_aux, coords[slot_index, 0], block_edge) for slot_index in range(slot_count)
    ]
    terms_i = []
    terms_j = []
    for slot_index in range(slot_count):
        term_i, term_j = second_mode(
            blocks[0, 0, slot_index],
            contractions[slot_index],
            aux_blocks[slot_index],
            first_rows[slot_index],
        )
        terms_i.append(term_i)
        terms_j.append(term_j)
    orbital_ids = jnp.arange(orbital_rows // block_edge, dtype=jnp.int32)[:, None]
    onehot_i = (orbital_ids == coords[None, :, 1]).astype(jnp.float32) * weights[None, :]
    onehot_j = (orbital_ids == coords[None, :, 2]).astype(jnp.float32) * weights[None, :]
    orbital_sum = jnp.einsum("bs,ser->ber", onehot_i, jnp.stack(terms_i), precision=precise_level)
    orbital_sum = orbital_sum + jnp.einsum(
        "bs,ser->ber", onehot_j, jnp.stack(terms_j), precision=precise_level
    )
    orbital_sum = orbital_sum.reshape(orbital_rows, factor_rank)
    share_rows = orbital_rows // lax.axis_size("narrow")
    summed = lax.psum(orbital_sum, ("wide", "narrow"))
    owned_orbital = lax.dynamic_slice_in_dim(
        summed, lax.axis_index("narrow") * share_rows, share_rows, 0
    )
    orbital_new = product(owned_orbital, inverse_of(2.0 * gram_a * gram_b))
    return (aux_owned[None], orbital_new)


def solution(mesh):
    return jax.shard_map(
        on_device,
        mesh=mesh,
        in_specs=(
            P("wide", "narrow", None, None, None),
            P("wide", "narrow", None, None),
            P("wide", "narrow"),
            P("narrow", None),
        ),
        out_specs=(P("narrow", "wide", None), P("narrow", None)),
        check_vma=False,
    )
```

profile of v0, /device:TPU:1, one launch (start us, length us, event | category | flops | bytes accessed | tf_op | source)
XLA Modules:
  0.0 673.6 jit_solution(5597649418127929185)
XLA Ops:
  13.2 3.4 slice_bitcast_fusion.1
  16.6 2.2 reshape_squeeze.6
  18.8 2.0 reshape_squeeze.7
  21.4 3.1 copy.32
  24.5 1.9 copy.33
  26.7 32.2 %all-gather.2.cloned.1.call-done = f32[4096,128]{1,0:T(8,128)} async-done(((f32[256,128]{1,0:T(8,128)}), f32[4096,128]{1,0:T(8,128)}) %all-gather.2.cloned.1.call-update) | async-done | bytes 2097168 | tf_op jit(solution)/shard_map/all_gather | solution.py:44
  58.9 5.0 convolution_bitcast_fusion.1
  63.9 2.9 copy.26
  66.8 4.1 convolution_bitcast_fusion
  70.9 1.9 copy.27
  73.6 2.3 multiply_reduce_fusion.4
  78.0 5.7 fusion.59
  83.8 11.7 %cholesky.44 = f32[128,128]{1,0:T(8,128)S(1)} custom-call(f32[128,128]{1,0:T(8,128)S(1)} %fusion.26), custom_call_target="Cholesky" | custom-call | tf_op jit(solution)/shard_map/jit(cholesky)/cholesky | solution.py:17
  96.8 9.8 %custom-call.8 = f32[1,128,128]{1,2,0:T(8,128)S(1)} custom-call(f32[1,128,128]{2,1,0:T(8,128)S(1)} %fusion.6), custom_call_target="InvertDiagBlocksLowerTriangular" | custom-call | tf_op jit(solution)/shard_map/jit(_cho_solve)/triangular_solve | solution.py:18
  107.2 184.8 %reduce-scatter.2.cloned.1.call-done = f32[32,128]{1,0:T(8,128)} async-done(((f32[1024,128]{1,0:T(8,128)}), f32[32,128]{1,0:T(8,128)}) %reduce-scatter.2.cloned.1.call-update) | async-done | bytes 16400 | tf_op jit(solution)/shard_map/reduce_scatter | solution.py:68
  293.0 35.9 %all_gather.7 = f32[1024,128]{1,0:T(8,128)S(1)} all-gather(f32[32,128]{1,0:T(8,128)S(1)} %fusion.60), channel_id=1, replica_groups=mesh['wide'=32,'narrow'=16] {'wide'}, dimensions={0}, use_global_device_ids=true | all-gather | bytes 540672 | tf_op jit(solution)/shard_map/all_gather | solution.py:71
  329.8 1.8 multiply_reduce_fusion.3
  335.5 1.9 fusion.12
  337.4 2.0 convolution_add_fusion
  339.4 2.5 copy.34
  341.9 298.8 %all-reduce.3.cloned.1.call-done = (f32[128,128]{0,1:T(8,128)}, f32[4096,128]{1,0:T(8,128)}) async-done(((f32[128,128]{0,1:T(8,128)}, f32[4096,128]{1,0:T(8,128)}), (f32[128,128]{0,1:T(8,128)}, f32[4096,128]{1,0:T(8,128)})) %all-reduce.3.cloned.1.call-update) | async-done | bytes 2162704 | tf_op jit(solution)/shard_map/psum | solution.py:70
  641.7 12.0 %cholesky.55 = f32[128,128]{1,0:T(8,128)S(1)} custom-call(f32[128,128]{1,0:T(8,128)S(1)} %fusion.22), custom_call_target="Cholesky" | custom-call | tf_op jit(solution)/shard_map/jit(cholesky)/cholesky | solution.py:17
  654.9 9.8 %custom-call.9 = f32[1,128,128]{1,2,0:T(8,128)S(1)} custom-call(f32[1,128,128]{2,1,0:T(8,128)S(1)} %fusion.7), custom_call_target="InvertDiagBlocksLowerTriangular" | custom-call | tf_op jit(solution)/shard_map/jit(_cho_solve)/triangular_solve | solution.py:18
  665.3 1.8 fusion
  (41 shorter events, 15.7 us)
Async XLA Ops:
  7.2 51.7 %all-gather.2.cloned.1.call-start = ((), (), s32[]{:S(2)}) async-start(), calls=%async_computation.1 | async-start | bytes 2228224 | tf_op jit(solution)/shard_map/all_gather | solution.py:44
  7.9 284.1 %reduce-scatter.2.cloned.1.call-start = ((), (), s32[]{:S(2)}) async-start(), calls=%async_computation.2 | async-start | bytes 540672 | tf_op jit(solution)/shard_map/reduce_scatter | solution.py:68
  24.5 1.9 copy-start.3
  77.7 562.9 %all-reduce.3.cloned.1.call-start = ((), (), s32[]{:S(2)}) async-start(), calls=%async_computation.3 | async-start | bytes 4325376 | tf_op jit(solution)/shard_map/psum | solution.py:70
  292.0 39.7 %copy-start.1 = (f32[4096,64]{1,0:T(8,128)S(1)}, f32[4096,64]{1,0:T(8,128)}, u32[]{:S(2)}) copy-start(f32[4096,64]{1,0:T(8,128)} %copy.32) | copy-start | bytes 3145732
  293.0 40.4 %copy-start.2 = (f32[32,128]{1,0:T(8,128)}, f32[32,128]{1,0:T(8,128)S(1)}, u32[]{:S(2)}) copy-start(f32[32,128]{1,0:T(8,128)S(1)} %fusion.60) | copy-start | bytes 49156
  331.6 2.0 copy-start
Sparse Core Ops, SparseCore 0:
  10.1 48.7 all-gather.1
  77.9 214.0 reduce-scatter.1
  342.0 298.5 all-reduce.2
where the time goes:
time: 675 us; the launch traced here: 674 us
  waiting for transfers between devices  516 us (76%)
  other arithmetic  51.2 us (8%)
  blocking collectives  35.9 us (5%)
  matrix products  27.8 us (4%)
  local copies, waits for them, and re-layouts  23.7 us (4%)
  between operations  18.3 us (3%)
    psum x1, waiting for transfers between devices, on_device(): gram_a = lax.psum(product(aux_owned.T, aux_owned), ('wide', 'narrow'))  299 us
    reduce_scatter x1, waiting for transfers between devices, on_device(): lax.psum_scatter(column_sum, 'wide', scatter_dimension=0, tiled=True)  185 us
    all_gather x1, blocking collectives, on_device(): column_aux = lax.all_gather(aux_owned, 'wide', axis=0, tiled=True)  35.9 us
    all_gather x1, waiting for transfers between devices, on_device(): full_orbital = lax.all_gather(orbital_factor, 'narrow', axis=0, tiled=True)  32.2 us
    another operation x6, other arithmetic, inverse_of(): lower = jnp.linalg.cholesky(gram)  25 us
    dot_general x8, matrix products, product(): jnp.dot(left, right, precision=precise_level, preferred_element_type=jnp....  22.1 us
    another operation x4, other arithmetic, inverse_of(): jax.scipy.linalg.cho_solve((lower, True), jnp.eye(gram.shape[0], dtype=gr...  20.9 us
  transfers between devices with their start and end apart: 3, of which 3 were waited for; matrix products, arithmetic and copies ran while one was open for 6% of the time, Pallas kernels for 0%

commit v1 on v0

v1 whole, which is shorter than its diff:
```python
import functools
import types

import jax
import jax.numpy as jnp
from jax import lax
from jax.experimental import pallas as pl
from jax.experimental.pallas import tpu as pltpu
from jax.sharding import PartitionSpec as P

NX, NY = 4, 8
NW = NX * NY
EDGE = 64
RANK = 128
HALVES = EDGE // NW
QB = 16
SPAN = EDGE * EDGE
CHUNK = 256
SUB = CHUNK // 2
F32, BF16 = jnp.float32, jnp.bfloat16
HIGHEST = lax.Precision.HIGHEST


def dot_full(left, right):
    return jnp.dot(left, right, precision=HIGHEST, preferred_element_type=F32)


def dot_fast(left, right):
    return jnp.dot(left, right, preferred_element_type=F32)


def pivot_step(rows):
    lane = lax.broadcasted_iota(jnp.int32, (8, RANK), 1)
    sub = lax.broadcasted_iota(jnp.int32, (8, RANK), 0)
    head = lane < 8

    def over_lanes(block, column):
        return jnp.broadcast_to(block[:, column : column + 1], (8, RANK))

    def over_rows(block, row):
        return jnp.broadcast_to(block[row : row + 1, :], (8, RANK))

    panel = rows[0]
    cols = [over_lanes(panel, m) for m in range(8)]
    for j in range(8):
        scale = 1.0 / over_rows(cols[j], j)
        fresh = []
        for m in range(8):
            if m == j:
                fresh.append(jnp.where(sub == j, scale, -cols[j] * scale))
            else:
                ratio = over_rows(cols[m], j) * scale
                fresh.append(jnp.where(sub == j, ratio, cols[m] - cols[j] * ratio))
        cols = fresh
    panel = jnp.where(head, jnp.where(lane == sub, 1.0, 0.0), panel)
    solved = cols[0] * over_rows(panel, 0)
    for m in range(1, 8):
        solved = solved + cols[m] * over_rows(panel, m)
    spread = [over_rows(solved, m) for m in range(8)]
    out = []
    for row in rows[1:]:
        total = jnp.where(head, 0.0, row)
        for m in range(8):
            total = total - over_lanes(row, m) * spread[m]
        out.append(total)
    out.append(solved)
    return tuple(pltpu.roll(block, RANK - 8, 1) for block in out)


def invert_steps(ref, first, last):
    rows = tuple(ref[8 * k : 8 * k + 8, :] for k in range(16))
    rows = lax.fori_loop(first, last, lambda t, held: pivot_step(held), rows)
    for k in range(16):
        ref[8 * k : 8 * k + 8, :] = rows[k]


def scratch_plan(nz):
    nc = 2 * nz
    vmem = dict(
        xs=((2, EDGE, SPAN), F32),
        xh=((2, EDGE, SPAN), BF16),
        xl=((2, EDGE, SPAN), BF16),
        xt=((2, SPAN, 3 * EDGE), BF16),
        full=((CHUNK * nc, RANK), F32),
        where=((4 * 8 * nz, RANK), F32),
        picks=((4 * EDGE, RANK), F32),
        krh=((SPAN, RANK), BF16),
        krl=((SPAN, RANK), BF16),
        gram=((RANK, RANK), F32),
        gram_in=((RANK, RANK), F32),
        gram_b=((RANK, RANK), F32),
        gram_own=((RANK, RANK), F32),
        gram_a=((RANK, RANK), F32),
        inv=((RANK, RANK), F32),
        meta=((16, RANK), F32),
        meta_x=((16 * NX, RANK), F32),
        metas=((16 * NW, RANK), F32),
        pick_aux_t=((4 * NW, RANK), F32),
        pick_aux=((RANK, 4 * NW), F32),
        pick_orb_t=((8 * NW, RANK), F32),
        pick_orb=((RANK, 8 * NW), F32),
        pick_reply=((8 * NW, RANK), F32),
        terms=((4 * EDGE, RANK), F32),
        fwd=((4 * NW, RANK), F32),
        fwd_mid=((4 * NW, RANK), F32),
        fwd_turn=((4 * NW, RANK), F32),
        fwd_in=((4 * NW, RANK), F32),
        rep=((8 * NW, RANK), F32),
        rep_mid=((8 * NW, RANK), F32),
        rep_turn=((8 * NW, RANK), F32),
        rep_in=((8 * NW, RANK), F32),
        own=((NW, RANK), F32),
        own_mid=((NW, RANK), F32),
        own_turn=((8 * NY, RANK), F32),
        own_in=((8 * NY, RANK), F32),
        tile=((8, RANK), F32),
        tile_core=((8, RANK), F32),
        tile_sum=((8, RANK), F32),
        tile_all=((8, RANK), F32),
        sum_own=((8, RANK), F32),
        tile_z=((8 * nz, RANK), F32),
        tile_y=((8 * NY, RANK), F32),
        tile_x=((8 * NW, RANK), F32),
        orb=((8 * NW, RANK), F32),
        orb_mid=((8 * NW, RANK), F32),
        orb_turn=((8 * NW, RANK), F32),
        orb_in=((8 * NW, RANK), F32),
        dense=((16 * nz, RANK), F32),
        dense_core=((8 * nz, RANK), F32),
        part=((8 * nz, RANK), F32),
        part_z=((8 * nz, RANK), F32),
        sum_y=((8 * NY, RANK), F32),
        sum_x=((8 * NW, RANK), F32),
        final=((8 * NW, RANK), F32),
    )
    sems = dict(
        load=1,
        up=8,
        down=8,
        across=16,
        grams=1,
        meta_sx=NX,
        meta_sy=NY,
        fwd_sx=NX,
        fwd_sy=NY,
        rep_sx=NX,
        rep_sy=NY,
        own_sx=NX,
        own_sy=NY,
        tile_sc=1,
        tile_sz=nz,
        tile_sy=NY,
        tile_sx=NX,
        orb_sx=NX,
        orb_sy=NY,
        dense_sc=1,
        part_sz=nz,
        sum_sy=NY,
        sum_sx=NX,
    )
    return vmem, sems


def kernel(nz, coords, count, b_in, blocks, aux_out, orb_out, *scratch):
    vmem, sems = scratch_plan(nz)
    m = types.SimpleNamespace(**dict(zip(vmem, scratch)))
    rest = scratch[len(vmem) :]
    sent = dict(zip(sems, rest[: len(sems)]))
    got = dict(zip(sems, rest[len(sems) :]))

    w = lax.axis_index("wide")
    c = lax.axis_index("narrow")
    x, y = w % NX, w // NX
    z, core = c // 2, c % 2
    pending = []

    def send(src, dst, name, index, wide=None, narrow=None):
        copy = pltpu.make_async_remote_copy(
            src_ref=src,
            dst_ref=dst,
            send_sem=sent[name].at[index],
            recv_sem=got[name].at[index],
            device_id=(w if wide is None else wide, c if narrow is None else narrow),
            device_id_type=pl.DeviceIdType.MESH,
        )
        copy.start()
        pending.append(copy)
        return copy

    def rows_of(ref, index, size):
        return ref.at[pl.ds(pl.multiple_of(index * size, 8), size)]

    def over_x(name, piece, dst, size):
        copies = []
        for d in range(1, NX):
            peer = (x + d) % NX
            copies.append(send(piece(peer), rows_of(dst, x, size), name, d, wide=y * NX + peer))
        return copies

    def over_y(name, piece, dst, size):
        copies = []
        for d in range(1, NY):
            peer = (y + d) % NY
            copies.append(send(piece(peer), rows_of(dst, y, size), name, d, wide=peer * NX + x))
        return copies

    def over_z(name, piece, dst, size):
        copies = []
        for d in range(1, nz):
            peer = (z + d) % nz
            copies.append(send(piece(peer), rows_of(dst, z, size), name, d, narrow=peer * 2 + core))
        return copies

    def arrived(copies):
        for copy in copies:
            copy.wait_recv()

    def keep(dst, index, size, src, src_index):
        dst[pl.ds(pl.multiple_of(index * size, 8), size), :] = src[
            pl.ds(pl.multiple_of(src_index * size, 8), size), :
        ]

    load = pltpu.make_async_copy(blocks, m.xs, sent["load"].at[0])
    load.start()

    barrier = pltpu.get_barrier_semaphore()
    for d in range(1, NX):
        pl.semaphore_signal(
            barrier, inc=1, device_id=(y * NX + (x + d) % NX, c), device_id_type=pl.DeviceIdType.MESH
        )
    for d in range(1, NY):
        pl.semaphore_signal(
            barrier, inc=1, device_id=((y + d) % NY * NX + x, c), device_id_type=pl.DeviceIdType.MESH
        )
    for d in range(1, nz):
        pl.semaphore_signal(
            barrier, inc=1, device_id=(w, (z + d) % nz * 2 + core), device_id_type=pl.DeviceIdType.MESH
        )
    partner = z * 2 + 1 - core
    pl.semaphore_signal(barrier, inc=1, device_id=(w, partner), device_id_type=pl.DeviceIdType.MESH)

    lane = lax.broadcasted_iota(jnp.int32, (8, RANK), 1)
    row = lax.broadcasted_iota(jnp.int32, (8, RANK), 0)
    live = [jnp.where(count[0, 0] > s, 1.0, 0.0) for s in range(2)]
    low = jnp.zeros((8, RANK), F32)
    high = jnp.zeros((8, RANK), F32)
    for s in range(2):
        for h in range(HALVES):
            hit = (row == 2 * s + h) & (lane == h * QB + coords[s, 0])
            low = low + jnp.where(hit, live[s], 0.0)
            for side in range(2):
                b = coords[s, 1 + side]
                spot = (b // 4 % 2) * (8 * nz) + (b // 8) * 8 + h * 4 + b % 4
                hit = (row == 2 * (2 * s + side) + h) & (lane == spot)
                high = high + jnp.where(hit, live[s], 0.0)
    blocks_all = 8 * nz
    block_id = lax.broadcasted_iota(jnp.int32, (blocks_all, RANK), 0)
    for t in range(4):
        m.where[blocks_all * t : blocks_all * (t + 1), :] = jnp.where(
            block_id == coords[t // 2, 1 + t % 2], 1.0, 0.0
        )
    m.picks[...] = jnp.zeros_like(m.picks)
    m.meta[0:8, :] = low
    m.meta[8:16, :] = high
    m.full[pl.ds(pl.multiple_of(c * CHUNK, CHUNK), CHUNK), :] = b_in[...]
    m.meta_x[pl.ds(pl.multiple_of(x * 16, 16), 16), :] = m.meta[...]

    pl.semaphore_wait(barrier, NX + NY + nz - 3 + 1)

    def piece_at(step, part, back):
        origin = (z + step) % nz if back else (z - step + nz) % nz
        return m.full.at[
            pl.ds(pl.multiple_of((origin * 2 + core) * CHUNK + part * SUB, SUB), SUB)
        ]

    def hop(step, part, back):
        peer = (z - 1 + nz) % nz if back else (z + 1) % nz
        src = b_in.at[pl.ds(part * SUB, SUB)] if step == 0 else piece_at(step, part, back)
        return send(
            src,
            piece_at(step, part, back),
            "down" if back else "up",
            2 * step + part,
            narrow=peer * 2 + core,
        )

    across = []

    def to_partner(step, part, back):
        src = b_in.at[pl.ds(part * SUB, SUB)] if step == 0 else piece_at(step, part, back)
        across.append(send(src, piece_at(step, part, back), "across", len(across), narrow=partner))

    half_way = nz // 2

    def parts_of(step, back):
        if step < half_way:
            return (0, 1)
        return (1,) if back else (0,)

    hops = {}
    for part in (0, 1):
        for back in (False, True):
            if part in parts_of(1, back):
                hops[1, part, back] = hop(0, part, back)
    meta_x = over_x("meta_sx", lambda peer: m.meta, m.meta_x, 16)
    for part in (0, 1):
        to_partner(0, part, False)

    own_chunk = b_in[...]
    m.gram[...] = dot_full(own_chunk.T, own_chunk)

    def prepare(slot, first, last):
        def one(t, carry):
            span = pl.ds(pl.multiple_of(t * RANK, RANK), RANK)
            part = m.xs[slot, :, span]
            top = part.astype(BF16)
            rest = part - top.astype(F32)
            m.xh[slot, :, span] = top
            m.xl[slot, :, span] = rest.astype(BF16)
            wide_top = top.astype(F32)
            turned = jnp.concatenate([wide_top, rest, wide_top], axis=0).T
            m.xt[slot, span, :] = turned.astype(BF16)
            return carry

        lax.fori_loop(first, last, one, 0)

    load.wait()
    pieces = SPAN // RANK
    prepare(0, 0, pieces // 4)
    quarter = pieces // 2
    jobs = [
        lambda: prepare(0, pieces // 4, pieces * 3 // 4),
        lambda: (prepare(0, pieces * 3 // 4, pieces), prepare(1, 0, pieces // 4)),
        lambda: prepare(1, pieces // 4, pieces * 3 // 4),
        lambda: prepare(1, pieces * 3 // 4, pieces),
    ]

    def add_gram(origin):
        chunk = m.full[pl.ds(pl.multiple_of((origin * 2 + core) * CHUNK, CHUNK), CHUNK), :]
        m.gram[...] += dot_full(chunk.T, chunk)

    def pick_chunk(chunk):
        for b in range(4):
            held = m.full[pl.ds(pl.multiple_of(chunk * CHUNK + b * EDGE, EDGE), EDGE), :]
            for t in range(4):
                m.picks[EDGE * t : EDGE * t + EDGE, :] += (
                    m.where[pl.ds(blocks_all * t + chunk * 4 + b, 1), :] * held
                )

    def pick_partner(step):
        first, last = (0, 2) if step == 0 else (4 * step - 2, min(4 * step + 2, 4 * half_way))
        arrived(across[first:last])
        pick_chunk((z + step) % nz * 2 + 1 - core)
        if 0 < step < half_way:
            pick_chunk((z - step + nz) % nz * 2 + 1 - core)

    pick_chunk(c)
    meta_y = None
    for step in range(1, half_way + 1):
        for part in (0, 1):
            for back in (False, True):
                if part not in parts_of(step, back):
                    continue
                hops[step, part, back].wait_recv()
                if step < half_way and part in parts_of(step + 1, back):
                    hops[step + 1, part, back] = hop(step, part, back)
                to_partner(step, part, back)
        if step == 1:
            arrived(meta_x)
            meta_y = over_y("meta_sy", lambda peer: m.meta_x, m.metas, 16 * NX)
            m.metas[pl.ds(pl.multiple_of(y * 16 * NX, 16 * NX), 16 * NX), :] = m.meta_x[...]
        add_gram((z + step) % nz)
        pick_chunk((z + step) % nz * 2 + core)
        if step < half_way:
            add_gram((z - step + nz) % nz)
            pick_chunk((z - step + nz) % nz * 2 + core)
        pick_partner(step - 1)
        if jobs:
            jobs.pop(0)()
    while jobs:
        jobs.pop(0)()

    grams = send(m.gram, m.gram_in, "grams", 0, narrow=partner)
    arrived(meta_y)
    for yy in range(NY):
        for xx in range(NX):
            at, turn = yy * NX + xx, xx * NY + yy
            tile = m.metas[16 * at : 16 * at + 8, :]
            m.pick_aux_t[4 * at : 4 * at + 4, :] = m.metas[16 * at : 16 * at + 4, :]
            m.pick_reply[8 * turn : 8 * turn + 8, :] = tile
            m.pick_orb_t[8 * at : 8 * at + 8, :] = m.metas[16 * at + 8 : 16 * at + 16, :]
    m.pick_aux[...] = m.pick_aux_t[...].T
    m.pick_orb[...] = m.pick_orb_t[...].T
    pick_partner(half_way)

    def block_rows(s, side):
        return m.picks[EDGE * (2 * s + side) : EDGE * (2 * s + side + 1), :]

    def eight_rows(s, t):
        return m.picks[pl.ds(pl.multiple_of(2 * EDGE * s + t * 8, 8), 8), :]

    for s in range(2):
        rows_j = block_rows(s, 1)

        def pairs(t, carry, s=s, rows_j=rows_j):
            span = pl.ds(pl.multiple_of(t * 512, 512), 512)
            both = (eight_rows(s, t)[:, None, :] * rows_j[None]).reshape(512, RANK)
            top = both.astype(BF16)
            m.krh[span, :] = top
            m.krl[span, :] = (both - top.astype(F32)).astype(BF16)
            return carry

        lax.fori_loop(0, 8, pairs, 0)
        m.terms[EDGE * s : EDGE * s + EDGE, :] = (
            dot_fast(m.xh[s], m.krh[...])
            + dot_fast(m.xh[s], m.krl[...])
            + dot_fast(m.xl[s], m.krh[...])
        )

    for xx in range(NX):
        for s in range(2):
            for h in range(HALVES):
                m.fwd[pl.ds(4 * NY * xx + 2 * s + h, NY, stride=4), :] = m.terms[
                    pl.ds(EDGE * s + NW * h + xx, NY, stride=NX), :
                ]
    size = 4 * NY
    fwd_x = over_x("fwd_sx", lambda peer: rows_of(m.fwd, peer, size), m.fwd_mid, size)
    keep(m.fwd_mid, x, size, m.fwd, x)

    grams.wait_recv()
    m.gram_b[...] = m.gram[...] + m.gram_in[...]
    m.inv[...] = m.gram_b[...] * m.gram_b[...]
    invert_steps(m.inv, 0, 5)

    def turn_around(mid, turned, size):
        for xx in range(NX):
            for yy in range(NY):
                to, at = yy * NX + xx, xx * NY + yy
                turned[size * to : size * to + size, :] = mid[size * at : size * at + size, :]

    arrived(fwd_x)
    turn_around(m.fwd_mid, m.fwd_turn, 4)
    size = 4 * NX
    fwd_y = over_y("fwd_sy", lambda peer: rows_of(m.fwd_turn, peer, 4 * NX), m.fwd_in, size)
    keep(m.fwd_in, y, size, m.fwd_turn, y)
    invert_steps(m.inv, 5, 16)
    arrived(fwd_y)

    aux_sum = dot_full(m.pick_aux[0 : HALVES * QB, :], m.fwd_in[...])
    aux_own = dot_full(aux_sum, m.inv[...])

    m.rep[...] = dot_full(m.pick_reply[:, 0 : HALVES * QB], aux_own)
    m.gram_own[...] = dot_full(aux_own.T, aux_own)
    for xx in range(NX):
        for yy in range(NY):
            at, source = 8 * (xx * NY + yy) + 4, 4 * (yy * NX + xx)
            m.rep[at : at + 4, :] = m.gram_own[source : source + 4, :]
    size = 8 * NY
    rep_x = over_x("rep_sx", lambda peer: rows_of(m.rep, peer, 8 * NY), m.rep_mid, size)
    keep(m.rep_mid, x, size, m.rep, x)

    to = lax.broadcasted_iota(jnp.int32, (NW, HALVES * QB), 0)
    what = lax.broadcasted_iota(jnp.int32, (NW, HALVES * QB), 1)
    target = (to % NY) * NX + to // NY
    share = jnp.where(what == target % 2 * QB + target // 2, 1.0, 0.0)
    m.own[...] = dot_full(share, aux_own)
    own_x = over_x("own_sx", lambda peer: rows_of(m.own, peer, NY), m.own_mid, NY)
    keep(m.own_mid, x, NY, m.own, x)

    arrived(rep_x)
    turn_around(m.rep_mid, m.rep_turn, 8)
    size = 8 * NX
    rep_y = over_y("rep_sy", lambda peer: rows_of(m.rep_turn, peer, 8 * NX), m.rep_in, size)
    keep(m.rep_in, y, size, m.rep_turn, y)

    arrived(own_x)
    m.own_turn[...] = jnp.zeros_like(m.own_turn)
    for xx in range(NX):
        m.own_turn[pl.ds(xx, NY, stride=8), :] = m.own_mid[NY * xx : NY * xx + NY, :]
    own_y = over_y("own_sy", lambda peer: rows_of(m.own_turn, peer, 8), m.own_in, 8)
    keep(m.own_in, y, 8, m.own_turn, y)

    arrived(rep_y)
    total = m.rep_in[0:8, :]
    for k in range(1, NW):
        total = total + m.rep_in[8 * k : 8 * k + 8, :]
    m.tile[...] = total
    tile_core = send(m.tile, m.tile_core, "tile_sc", 0, narrow=partner)

    for s in range(2):
        aux_rows = jnp.concatenate(
            [m.rep_in[pl.ds(2 * s + h, NW, stride=8), :] for h in range(HALVES)], axis=0
        )
        top = aux_rows.astype(BF16)
        rest = (aux_rows - top.astype(F32)).astype(BF16)
        stacked = jnp.concatenate([top, top, rest], axis=0)
        rows_j = block_rows(s, 1)

        def sums(t, term_j, s=s, stacked=stacked, rows_j=rows_j):
            spread = dot_fast(m.xt[s, pl.ds(pl.multiple_of(t * 512, 512), 512), :], stacked)
            spread = spread.reshape(8, EDGE, RANK)
            m.terms[pl.ds(pl.multiple_of(2 * EDGE * s + t * 8, 8), 8), :] = jnp.sum(
                spread * rows_j[None], axis=1
            )
            return term_j + jnp.sum(spread * eight_rows(s, t)[:, None, :], axis=0)

        term_j = lax.fori_loop(0, 8, sums, jnp.zeros((EDGE, RANK), F32))
        m.terms[EDGE * (2 * s + 1) : EDGE * (2 * s + 2), :] = term_j
        for xx in range(NX):
            for side in range(2):
                for h in range(HALVES):
                    block = 2 * s + side
                    m.orb[pl.ds(8 * NY * xx + 2 * block + h, NY, stride=8), :] = m.terms[
                        pl.ds(EDGE * block + NW * h + xx, NY, stride=NX), :
                    ]
        if s == 0:
            tile_core.wait_recv()
            m.tile_sum[...] = m.tile[...] + m.tile_core[...]
            tile_z = over_z("tile_sz", lambda peer: m.tile_sum, m.tile_z, 8)
            m.tile_z[pl.ds(pl.multiple_of(z * 8, 8), 8), :] = m.tile_sum[...]
    size = 8 * NY
    orb_x = over_x("orb_sx", lambda peer: rows_of(m.orb, peer, 8 * NY), m.orb_mid, size)
    keep(m.orb_mid, x, size, m.orb, x)

    arrived(tile_z)
    total = m.tile_z[0:8, :]
    for k in range(1, nz):
        total = total + m.tile_z[8 * k : 8 * k + 8, :]
    m.tile_all[...] = total
    tile_y = over_y("tile_sy", lambda peer: m.tile_all, m.tile_y, 8)
    m.tile_y[pl.ds(pl.multiple_of(y * 8, 8), 8), :] = total

    arrived(orb_x)
    turn_around(m.orb_mid, m.orb_turn, 8)
    size = 8 * NX
    orb_y = over_y("orb_sy", lambda peer: rows_of(m.orb_turn, peer, 8 * NX), m.orb_in, size)
    keep(m.orb_in, y, size, m.orb_turn, y)

    arrived(own_y)
    for yy in range(NY):
        aux_out[NX * yy : NX * yy + NX, :] = m.own_in[8 * yy : 8 * yy + NX, :]

    arrived(tile_y)
    size = 8 * NY
    tile_x = over_x("tile_sx", lambda peer: m.tile_y, m.tile_x, size)
    m.tile_x[pl.ds(pl.multiple_of(x * size, 8), size), :] = m.tile_y[...]

    arrived(orb_y)
    m.dense[...] = dot_full(m.pick_orb[0 : 16 * nz, :], m.orb_in[...])
    size = 8 * nz
    dense_core = send(rows_of(m.dense, 1 - core, size), m.dense_core, "dense_sc", 0, narrow=partner)
    dense_core.wait_recv()
    m.part[...] = m.dense[pl.ds(pl.multiple_of(core * size, 8), size), :] + m.dense_core[...]
    part_z = over_z("part_sz", lambda peer: rows_of(m.part, peer, 8), m.part_z, 8)
    keep(m.part_z, z, 8, m.part, z)

    arrived(tile_x)
    for xx in range(NX):
        for yy in range(NY):
            at, to_row = 8 * (xx * NY + yy) + 4, 4 * (yy * NX + xx)
            m.gram_a[to_row : to_row + 4, :] = m.tile_x[at : at + 4, :]
    m.inv[...] = 2.0 * m.gram_a[...] * m.gram_b[...]
    invert_steps(m.inv, 0, 8)

    arrived(part_z)
    total = m.part_z[0:8, :]
    for k in range(1, nz):
        total = total + m.part_z[8 * k : 8 * k + 8, :]
    m.sum_own[...] = total
    sum_y = over_y("sum_sy", lambda peer: m.sum_own, m.sum_y, 8)
    m.sum_y[pl.ds(pl.multiple_of(y * 8, 8), 8), :] = total
    invert_steps(m.inv, 8, 16)
    arrived(sum_y)
    size = 8 * NY
    sum_x = over_x("sum_sx", lambda peer: m.sum_y, m.sum_x, size)
    m.sum_x[pl.ds(pl.multiple_of(x * size, 8), size), :] = m.sum_y[...]
    arrived(sum_x)
    m.final[...] = dot_full(m.sum_x[...], m.inv[...])
    for xx in range(NX):
        for b in range(4):
            for h in range(HALVES):
                orb_out[pl.ds(EDGE * b + NW * h + xx, NY, stride=NX), :] = m.final[
                    pl.ds(8 * NY * xx + 4 * h + b, NY, stride=8), :
                ]
    for copy in pending:
        copy.wait_send()


def on_device(blocks, block_coords, block_count, orbital_factor, *, nz):
    vmem, sems = scratch_plan(nz)
    scratch = [pltpu.VMEM(shape, dtype) for shape, dtype in vmem.values()]
    scratch += [pltpu.SemaphoreType.DMA((n,)) for n in sems.values()] * 2
    aux, orbital = pl.pallas_call(
        functools.partial(kernel, nz),
        out_shape=(
            jax.ShapeDtypeStruct((NW, RANK), F32),
            jax.ShapeDtypeStruct((CHUNK, RANK), F32),
        ),
        in_specs=[
            pl.BlockSpec(memory_space=pltpu.SMEM),
            pl.BlockSpec(memory_space=pltpu.SMEM),
            pl.BlockSpec(memory_space=pltpu.VMEM),
            pl.BlockSpec(memory_space=pl.ANY),
        ],
        out_specs=(
            pl.BlockSpec(memory_space=pltpu.VMEM),
            pl.BlockSpec(memory_space=pltpu.VMEM),
        ),
        scratch_shapes=scratch,
        compiler_params=pltpu.CompilerParams(
            collective_id=0, has_side_effects=True, vmem_limit_bytes=48 << 20
        ),
    )(
        block_coords.reshape(2, 3),
        block_count.reshape(1, 1),
        orbital_factor,
        blocks.reshape(2, EDGE, SPAN),
    )
    return aux[None], orbital


def solution(mesh):
    return jax.shard_map(
        functools.partial(on_device, nz=mesh.shape["narrow"] // 2),
        mesh=mesh,
        in_specs=(
            P("wide", "narrow", None, None, None),
            P("wide", "narrow", None, None),
            P("wide", "narrow"),
            P("narrow", None),
        ),
        out_specs=(P("narrow", "wide", None), P("narrow", None)),
        check_vma=False,
    )
```

time: 675 us -> 90.7 us (0.13)
  waiting for transfers between devices: 516 us -> 0 us
  Pallas kernels: 0 us -> 84.8 us
  other arithmetic: 51.2 us -> 0 us
  blocking collectives: 35.9 us -> 0 us
  matrix products: 27.8 us -> 0 us
  local copies, waits for them, and re-layouts: 23.7 us -> 4.43 us
  between operations: 18.3 us -> 1.3 us
    psum x1 -> x0, waiting for transfers between devices: 299 us -> none  [on_device(): gram_a = lax.psum(product(aux_owned.T, aux_owned), ('wide', 'narrow'))]
    reduce_scatter x1 -> x0, waiting for transfers between devices: 185 us -> none  [on_device(): lax.psum_scatter(column_sum, 'wide', scatter_dimension=0, tiled=True)]
    pallas_call x0 -> x1, Pallas kernels: none -> 84.8 us  [on_device(): pl.pallas_call(functools.partial(kernel, nz), out_shape=(jax.ShapeDtypeSt...]
    another operation x10 -> x0, other arithmetic: 45.9 us -> none  [the longest x6 25 us: inverse_of(): lower = jnp.linalg.cholesky(gram)]
    all_gather x1 -> x0, blocking collectives: 35.9 us -> none  [on_device(): column_aux = lax.all_gather(aux_owned, 'wide', axis=0, tiled=True)]
    all_gather x1 -> x0, waiting for transfers between devices: 32.2 us -> none  [on_device(): full_orbital = lax.all_gather(orbital_factor, 'narrow', axis=0, tiled=True)]
    dot_general x11 -> x0, matrix products: 26.8 us -> none  [the longest x8 22.1 us: product(): jnp.dot(left, right, precision=precise_level, preferred_element_type=jnp....]
    dot_general x6 -> x0, local copies, waits for them, and re-layouts: 14.3 us -> none  [the longest x5 13.3 us: product(): jnp.dot(left, right, precision=precise_level, preferred_element_type=jnp....]
  transfers between devices with their start and end apart: 3 -> 0, of which waited for: 3 -> 0; matrix products, arithmetic and copies ran while one was open for 6% -> 0% of each run, Pallas kernels for 0% -> 0%
where the time goes in v1:
time: 90.7 us; the launch traced here: 90.5 us
  Pallas kernels  84.8 us (93%)
  local copies, waits for them, and re-layouts  4.43 us (5%)
  between operations  1.3 us (1%)
    pallas_call x1, Pallas kernels, on_device(): pl.pallas_call(functools.partial(kernel, nz), out_shape=(jax.ShapeDtypeSt...  84.8 us
    unnamed x8, local copies, waits for them, and re-layouts  4.43 us

profile of v1, /device:TPU:1, one launch (start us, length us, event | category | flops | bytes accessed | tf_op | source)
XLA Modules:
  0.0 90.5 jit_solution(14333183631170753978)
XLA Ops:
  1.3 0.0 copy-start
  1.3 1.6 %copy-done = f32[1,1,2,64,4096]{4,3,2,1,0:T(8,128)S(1)} copy-done((f32[1,1,2,64,4096]{4,3,2,1,0:T(8,128)S(1)}, f32[1,1,2,64,4096]{4,3,2,1,0:T(8,128)}, u32[]{:S(2)}) %copy-start) | copy-done | bytes 2097176
  2.9 0.0 copy-start.1
  2.9 0.9 copy-done.1
  3.8 0.0 copy-start.2
  3.8 0.7 copy-done.2
  4.5 84.8 %shard_map.59 = (f32[32,128]{1,0:T(8,128)S(1)}, f32[256,128]{1,0:T(8,128)S(1)}) custom-call(s32[2,3]{1,0:T(2,128)S(1)} %bitcast.5, s32[1,1]{1,0:T(1,128)S(6)} %copy.8.count, f32[256,128]{1,0:T(8,128)S(1)} %copy-done.1, f32[2,64,4096]{2,1,0:T(8,128)S(1)} %bitcast.3), custom_call_target="tpu_custom_call" | custom-call | tf_op jit(solution)/shard_map/pallas_call | solution.py:593
  89.2 0.6 copy.9
  89.8 0.7 copy.10
Async XLA Ops:
  1.3 1.6 %copy-start = (f32[1,1,2,64,4096]{4,3,2,1,0:T(8,128)S(1)}, f32[1,1,2,64,4096]{4,3,2,1,0:T(8,128)}, u32[]{:S(2)}) copy-start(f32[1,1,2,64,4096]{4,3,2,1,0:T(8,128)} %param.4) | copy-start | bytes 6291460
  2.9 0.9 copy-start.1
  3.8 0.7 copy-start.2

commit v2 on v1

--- a/solution.py
+++ b/solution.py
@@ -92,22 +92,24 @@
         gram_own=((RANK, RANK), F32),
         gram_a=((RANK, RANK), F32),
         inv=((RANK, RANK), F32),
-        meta=((16, RANK), F32),
-        meta_x=((16 * NX, RANK), F32),
-        metas=((16 * NW, RANK), F32),
+        where_at=((2, 3), jnp.int32),
+        lived=((1, 1), jnp.int32),
+        mine=((CHUNK, RANK), F32),
+        meta=((8, RANK), F32),
+        meta_x=((8 * NX, RANK), F32),
+        meta_row=((8, RANK), F32),
+        metas=((8 * NY, RANK), F32),
+        spread=((SPAN, RANK), F32),
         pick_aux_t=((4 * NW, RANK), F32),
         pick_aux=((RANK, 4 * NW), F32),
         pick_orb_t=((8 * NW, RANK), F32),
         pick_orb=((RANK, 8 * NW), F32),
         pick_reply=((8 * NW, RANK), F32),
         terms=((4 * EDGE, RANK), F32),
-        fwd=((4 * NW, RANK), F32),
-        fwd_mid=((4 * NW, RANK), F32),
-        fwd_turn=((4 * NW, RANK), F32),
-        fwd_in=((4 * NW, RANK), F32),
+        fwd=((NW, 4, RANK), F32),
+        fwd_in=((NW, 4, RANK), F32),
+        fwd_rows=((4 * NW, RANK), F32),
         rep=((8 * NW, RANK), F32),
-        rep_mid=((8 * NW, RANK), F32),
-        rep_turn=((8 * NW, RANK), F32),
         rep_in=((8 * NW, RANK), F32),
         own=((NW, RANK), F32),
         own_mid=((NW, RANK), F32),
@@ -122,8 +124,6 @@
         tile_y=((8 * NY, RANK), F32),
         tile_x=((8 * NW, RANK), F32),
         orb=((8 * NW, RANK), F32),
-        orb_mid=((8 * NW, RANK), F32),
-        orb_turn=((8 * NW, RANK), F32),
         orb_in=((8 * NW, RANK), F32),
         dense=((16 * nz, RANK), F32),
         dense_core=((8 * nz, RANK), F32),
@@ -134,25 +134,22 @@
         final=((8 * NW, RANK), F32),
     )
     sems = dict(
-        load=1,
+        load=4,
         up=8,
         down=8,
         across=16,
         grams=1,
         meta_sx=NX,
         meta_sy=NY,
-        fwd_sx=NX,
-        fwd_sy=NY,
-        rep_sx=NX,
-        rep_sy=NY,
+        fwd_s=1,
+        rep_s=1,
         own_sx=NX,
         own_sy=NY,
         tile_sc=1,
         tile_sz=nz,
         tile_sy=NY,
         tile_sx=NX,
-        orb_sx=NX,
-        orb_sy=NY,
+        orb_s=1,
         dense_sc=1,
         part_sz=nz,
         sum_sy=NY,
@@ -211,6 +208,24 @@
             copies.append(send(piece(peer), rows_of(dst, z, size), name, d, narrow=peer * 2 + core))
         return copies
 
+    def to_all(name, src_of, dst):
+        for dy in sorted(range(NY), key=lambda d: -min(d, NY - d)):
+            for dx in sorted(range(NX), key=lambda d: -min(d, NX - d)):
+                if dx or dy:
+                    peer = (y + dy) % NY * NX + (x + dx) % NX
+                    pltpu.make_async_remote_copy(
+                        src_ref=src_of(peer),
+                        dst_ref=dst,
+                        send_sem=sent[name].at[0],
+                        recv_sem=got[name].at[0],
+                        device_id=(peer, c),
+                        device_id_type=pl.DeviceIdType.MESH,
+                    ).start()
+
+    def all_in(name, others, which=None):
+        sem = (got if which is None else which)[name].at[0]
+        pltpu.make_async_copy(others, others, sem).wait()
+
     def arrived(copies):
         for copy in copies:
             copy.wait_recv()
@@ -220,8 +235,14 @@
             pl.ds(pl.multiple_of(src_index * size, 8), size), :
         ]
 
-    load = pltpu.make_async_copy(blocks, m.xs, sent["load"].at[0])
-    load.start()
+    loads = [
+        pltpu.make_async_copy(src, dst, sent["load"].at[k])
+        for k, (src, dst) in enumerate(
+            [(b_in, m.mine), (coords, m.where_at), (count, m.lived), (blocks, m.xs)]
+        )
+    ]
+    for copy in loads:
+        copy.start()
 
     barrier = pltpu.get_barrier_semaphore()
     for d in range(1, NX):
@@ -239,75 +260,31 @@
     partner = z * 2 + 1 - core
     pl.semaphore_signal(barrier, inc=1, device_id=(w, partner), device_id_type=pl.DeviceIdType.MESH)
 
+    m.picks[...] = jnp.zeros_like(m.picks)
+    m.pick_reply[...] = jnp.zeros_like(m.pick_reply)
+    m.meta_row[...] = jnp.zeros_like(m.meta_row)
+
+    loads[1].wait()
+    loads[2].wait()
     lane = lax.broadcasted_iota(jnp.int32, (8, RANK), 1)
-    row = lax.broadcasted_iota(jnp.int32, (8, RANK), 0)
-    live = [jnp.where(count[0, 0] > s, 1.0, 0.0) for s in range(2)]
-    low = jnp.zeros((8, RANK), F32)
-    high = jnp.zeros((8, RANK), F32)
-    for s in range(2):
-        for h in range(HALVES):
-            hit = (row == 2 * s + h) & (lane == h * QB + coords[s, 0])
-            low = low + jnp.where(hit, live[s], 0.0)
-            for side in range(2):
-                b = coords[s, 1 + side]
-                spot = (b // 4 % 2) * (8 * nz) + (b // 8) * 8 + h * 4 + b % 4
-                hit = (row == 2 * (2 * s + side) + h) & (lane == spot)
-                high = high + jnp.where(hit, live[s], 0.0)
     blocks_all = 8 * nz
     block_id = lax.broadcasted_iota(jnp.int32, (blocks_all, RANK), 0)
-    for t in range(4):
-        m.where[blocks_all * t : blocks_all * (t + 1), :] = jnp.where(
-            block_id == coords[t // 2, 1 + t % 2], 1.0, 0.0
-        )
-    m.picks[...] = jnp.zeros_like(m.picks)
-    m.meta[0:8, :] = low
-    m.meta[8:16, :] = high
-    m.full[pl.ds(pl.multiple_of(c * CHUNK, CHUNK), CHUNK), :] = b_in[...]
-    m.meta_x[pl.ds(pl.multiple_of(x * 16, 16), 16), :] = m.meta[...]
-
-    pl.semaphore_wait(barrier, NX + NY + nz - 3 + 1)
-
-    def piece_at(step, part, back):
-        origin = (z + step) % nz if back else (z - step + nz) % nz
-        return m.full.at[
-            pl.ds(pl.multiple_of((origin * 2 + core) * CHUNK + part * SUB, SUB), SUB)
-        ]
-
-    def hop(step, part, back):
-        peer = (z - 1 + nz) % nz if back else (z + 1) % nz
-        src = b_in.at[pl.ds(part * SUB, SUB)] if step == 0 else piece_at(step, part, back)
-        return send(
-            src,
-            piece_at(step, part, back),
-            "down" if back else "up",
-            2 * step + part,
-            narrow=peer * 2 + core,
-        )
-
-    across = []
-
-    def to_partner(step, part, back):
-        src = b_in.at[pl.ds(part * SUB, SUB)] if step == 0 else piece_at(step, part, back)
-        across.append(send(src, piece_at(step, part, back), "across", len(across), narrow=partner))
-
-    half_way = nz // 2
-
-    def parts_of(step, back):
-        if step < half_way:
-            return (0, 1)
-        return (1,) if back else (0,)
-
-    hops = {}
-    for part in (0, 1):
-        for back in (False, True):
-            if part in parts_of(1, back):
-                hops[1, part, back] = hop(0, part, back)
-    meta_x = over_x("meta_sx", lambda peer: m.meta, m.meta_x, 16)
-    for part in (0, 1):
-        to_partner(0, part, False)
-
-    own_chunk = b_in[...]
-    m.gram[...] = dot_full(own_chunk.T, own_chunk)
+    spots = jnp.zeros((8, RANK), F32)
+    for s in range(2):
+        live = jnp.broadcast_to(m.lived[0:1, 0:1], (8, RANK)) > s
+        for side in range(3):
+            at = jnp.broadcast_to(m.where_at[s : s + 1, side : side + 1], (8, RANK))
+            if side == 0:
+                t, spot = s, at
+            else:
+                t = 2 + 2 * s + side - 1
+                spot = (at & 7) // 4 * (8 * nz) + (at // 8) * 8 + (at & 3)
+                m.where[blocks_all * (t - 2) : blocks_all * (t - 1), :] = jnp.where(
+                    block_id == jnp.broadcast_to(at[0:1, :], block_id.shape), 1.0, 0.0
+                )
+            spot = jnp.where(live, spot, -1000).astype(F32)
+            spots = spots + jnp.where(lane == t, spot, 0.0)
+    m.meta[...] = spots
 
     def prepare(slot, first, last):
         def one(t, carry):
@@ -324,21 +301,6 @@
 
         lax.fori_loop(first, last, one, 0)
 
-    load.wait()
-    pieces = SPAN // RANK
-    prepare(0, 0, pieces // 4)
-    quarter = pieces // 2
-    jobs = [
-        lambda: prepare(0, pieces // 4, pieces * 3 // 4),
-        lambda: (prepare(0, pieces * 3 // 4, pieces), prepare(1, 0, pieces // 4)),
-        lambda: prepare(1, pieces // 4, pieces * 3 // 4),
-        lambda: prepare(1, pieces * 3 // 4, pieces),
-    ]
-
-    def add_gram(origin):
-        chunk = m.full[pl.ds(pl.multiple_of((origin * 2 + core) * CHUNK, CHUNK), CHUNK), :]
-        m.gram[...] += dot_full(chunk.T, chunk)
-
     def pick_chunk(chunk):
         for b in range(4):
             held = m.full[pl.ds(pl.multiple_of(chunk * CHUNK + b * EDGE, EDGE), EDGE), :]
@@ -347,6 +309,67 @@
                     m.where[pl.ds(blocks_all * t + chunk * 4 + b, 1), :] * held
                 )
 
+    loads[0].wait()
+    m.full[pl.ds(pl.multiple_of(c * CHUNK, CHUNK), CHUNK), :] = m.mine[...]
+    loads[3].wait()
+    pieces = SPAN // RANK
+    early = pieces // 2
+    prepare(0, 0, early)
+    pl.semaphore_wait(barrier, NX + NY + nz - 2)
+
+    def piece_at(step, part, back):
+        origin = (z + step) % nz if back else (z - step + nz) % nz
+        return m.full.at[
+            pl.ds(pl.multiple_of((origin * 2 + core) * CHUNK + part * SUB, SUB), SUB)
+        ]
+
+    def hop(step, part, back):
+        peer = (z - 1 + nz) % nz if back else (z + 1) % nz
+        src = m.mine.at[pl.ds(part * SUB, SUB)] if step == 0 else piece_at(step, part, back)
+        return send(
+            src,
+            piece_at(step, part, back),
+            "down" if back else "up",
+            2 * step + part,
+            narrow=peer * 2 + core,
+        )
+
+    across = []
+
+    def to_partner(step, part, back):
+        src = m.mine.at[pl.ds(part * SUB, SUB)] if step == 0 else piece_at(step, part, back)
+        across.append(send(src, piece_at(step, part, back), "across", len(across), narrow=partner))
+
+    half_way = nz // 2
+
+    def parts_of(step, back):
+        if step < half_way:
+            return (0, 1)
+        return (1,) if back else (0,)
+
+    hops = {}
+    for part in (0, 1):
+        for back in (False, True):
+            if part in parts_of(1, back):
+                hops[1, part, back] = hop(0, part, back)
+    meta_x = over_x("meta_sx", lambda peer: m.meta, m.meta_x, 8)
+    m.meta_x[pl.ds(pl.multiple_of(x * 8, 8), 8), :] = m.meta[...]
+    for part in (0, 1):
+        to_partner(0, part, False)
+    pick_chunk(c)
+    own_chunk = m.mine[...]
+    m.gram[...] = dot_full(own_chunk.T, own_chunk)
+    jobs = [
+        lambda: prepare(0, early, pieces),
+        lambda: prepare(1, 0, pieces // 3),
+        lambda: prepare(1, pieces // 3, pieces * 2 // 3),
+        lambda: prepare(1, pieces * 2 // 3, pieces),
+    ]
+
+    def add_gram(origin):
+        chunk = m.full[pl.ds(pl.multiple_of((origin * 2 + core) * CHUNK, CHUNK), CHUNK), :]
+        m.gram[...] += dot_full(chunk.T, chunk)
+
     def pick_partner(step):
         first, last = (0, 2) if step == 0 else (4 * step - 2, min(4 * step + 2, 4 * half_way))
         arrived(across[first:last])
@@ -354,7 +377,6 @@
         if 0 < step < half_way:
             pick_chunk((z - step + nz) % nz * 2 + 1 - core)
 
-    pick_chunk(c)
     meta_y = None
     for step in range(1, half_way + 1):
         for part in (0, 1):
@@ -367,8 +389,10 @@
                 to_partner(step, part, back)
         if step == 1:
             arrived(meta_x)
-            meta_y = over_y("meta_sy", lambda peer: m.meta_x, m.metas, 16 * NX)
-            m.metas[pl.ds(pl.multiple_of(y * 16 * NX, 16 * NX), 16 * NX), :] = m.meta_x[...]
+            for xx in range(NX):
+                m.meta_row[xx : xx + 1, :] = m.meta_x[8 * xx : 8 * xx + 1, :]
+            meta_y = over_y("meta_sy", lambda peer: m.meta_row, m.metas, 8)
+            m.metas[pl.ds(pl.multiple_of(y * 8, 8), 8), :] = m.meta_row[...]
         add_gram((z + step) % nz)
         pick_chunk((z + step) % nz * 2 + core)
         if step < half_way:
@@ -382,13 +406,19 @@
 
     grams = send(m.gram, m.gram_in, "grams", 0, narrow=partner)
     arrived(meta_y)
-    for yy in range(NY):
-        for xx in range(NX):
-            at, turn = yy * NX + xx, xx * NY + yy
-            tile = m.metas[16 * at : 16 * at + 8, :]
-            m.pick_aux_t[4 * at : 4 * at + 4, :] = m.metas[16 * at : 16 * at + 4, :]
-            m.pick_reply[8 * turn : 8 * turn + 8, :] = tile
-            m.pick_orb_t[8 * at : 8 * at + 8, :] = m.metas[16 * at + 8 : 16 * at + 16, :]
+    places = jnp.concatenate([m.metas[8 * yy : 8 * yy + NX, :] for yy in range(NY)], axis=0)
+    lanes = lax.broadcasted_iota(jnp.int32, (NW, RANK), 1).astype(F32)
+    for t in range(6):
+        place = jnp.broadcast_to(places[:, t : t + 1], (NW, RANK))
+        for h in range(HALVES):
+            if t < 2:
+                hot = jnp.where(lanes == place + QB * h, 1.0, 0.0)
+                m.pick_aux_t[pl.ds(2 * t + h, NW, stride=4), :] = hot
+                m.pick_reply[pl.ds(2 * t + h, NW, stride=8), :] = hot
+            else:
+                m.pick_orb_t[pl.ds(2 * (t - 2) + h, NW, stride=8), :] = jnp.where(
+                    lanes == place + 4 * h, 1.0, 0.0
+                )
     m.pick_aux[...] = m.pick_aux_t[...].T
     m.pick_orb[...] = m.pick_orb_t[...].T
     pick_partner(half_way)
@@ -417,47 +447,33 @@
             + dot_fast(m.xl[s], m.krh[...])
         )
 
-    for xx in range(NX):
-        for s in range(2):
-            for h in range(HALVES):
-                m.fwd[pl.ds(4 * NY * xx + 2 * s + h, NY, stride=4), :] = m.terms[
-                    pl.ds(EDGE * s + NW * h + xx, NY, stride=NX), :
-                ]
-    size = 4 * NY
-    fwd_x = over_x("fwd_sx", lambda peer: rows_of(m.fwd, peer, size), m.fwd_mid, size)
-    keep(m.fwd_mid, x, size, m.fwd, x)
+    for s in range(2):
+        for h in range(HALVES):
+            m.fwd_rows[pl.ds(2 * s + h, NW, stride=4), :] = m.terms[
+                EDGE * s + NW * h : EDGE * s + NW * (h + 1), :
+            ]
+    for k in range(NW):
+        m.fwd[k] = m.fwd_rows[4 * k : 4 * k + 4, :]
+    to_all("fwd_s", lambda peer: m.fwd.at[peer], m.fwd_in.at[w])
+    m.fwd_in[w] = m.fwd[w]
 
     grams.wait_recv()
     m.gram_b[...] = m.gram[...] + m.gram_in[...]
     m.inv[...] = m.gram_b[...] * m.gram_b[...]
-    invert_steps(m.inv, 0, 5)
-
-    def turn_around(mid, turned, size):
-        for xx in range(NX):
-            for yy in range(NY):
-                to, at = yy * NX + xx, xx * NY + yy
-                turned[size * to : size * to + size, :] = mid[size * at : size * at + size, :]
-
-    arrived(fwd_x)
-    turn_around(m.fwd_mid, m.fwd_turn, 4)
-    size = 4 * NX
-    fwd_y = over_y("fwd_sy", lambda peer: rows_of(m.fwd_turn, peer, 4 * NX), m.fwd_in, size)
-    keep(m.fwd_in, y, size, m.fwd_turn, y)
-    invert_steps(m.inv, 5, 16)
-    arrived(fwd_y)
-
-    aux_sum = dot_full(m.pick_aux[0 : HALVES * QB, :], m.fwd_in[...])
+    invert_steps(m.inv, 0, 16)
+    all_in("fwd_s", m.fwd_in.at[pl.ds(0, NW - 1)])
+    for k in range(NW):
+        m.fwd_rows[4 * k : 4 * k + 4, :] = m.fwd_in[k]
+
+    aux_sum = dot_full(m.pick_aux[0 : HALVES * QB, :], m.fwd_rows[...])
     aux_own = dot_full(aux_sum, m.inv[...])
 
     m.rep[...] = dot_full(m.pick_reply[:, 0 : HALVES * QB], aux_own)
     m.gram_own[...] = dot_full(aux_own.T, aux_own)
-    for xx in range(NX):
-        for yy in range(NY):
-            at, source = 8 * (xx * NY + yy) + 4, 4 * (yy * NX + xx)
-            m.rep[at : at + 4, :] = m.gram_own[source : source + 4, :]
-    size = 8 * NY
-    rep_x = over_x("rep_sx", lambda peer: rows_of(m.rep, peer, 8 * NY), m.rep_mid, size)
-    keep(m.rep_mid, x, size, m.rep, x)
+    for k in range(NW):
+        m.rep[8 * k + 4 : 8 * k + 8, :] = m.gram_own[4 * k : 4 * k + 4, :]
+    to_all("rep_s", lambda peer: rows_of(m.rep, peer, 8), rows_of(m.rep_in, w, 8))
+    keep(m.rep_in, w, 8, m.rep, w)
 
     to = lax.broadcasted_iota(jnp.int32, (NW, HALVES * QB), 0)
     what = lax.broadcasted_iota(jnp.int32, (NW, HALVES * QB), 1)
@@ -467,12 +483,6 @@
     own_x = over_x("own_sx", lambda peer: rows_of(m.own, peer, NY), m.own_mid, NY)
     keep(m.own_mid, x, NY, m.own, x)
 
-    arrived(rep_x)
-    turn_around(m.rep_mid, m.rep_turn, 8)
-    size = 8 * NX
-    rep_y = over_y("rep_sy", lambda peer: rows_of(m.rep_turn, peer, 8 * NX), m.rep_in, size)
-    keep(m.rep_in, y, size, m.rep_turn, y)
-
     arrived(own_x)
     m.own_turn[...] = jnp.zeros_like(m.own_turn)
     for xx in range(NX):
@@ -480,7 +490,7 @@
     own_y = over_y("own_sy", lambda peer: rows_of(m.own_turn, peer, 8), m.own_in, 8)
     keep(m.own_in, y, 8, m.own_turn, y)
 
-    arrived(rep_y)
+    all_in("rep_s", m.rep_in.at[pl.ds(0, 8 * (NW - 1))])
     total = m.rep_in[0:8, :]
     for k in range(1, NW):
         total = total + m.rep_in[8 * k : 8 * k + 8, :]
@@ -496,31 +506,33 @@
         stacked = jnp.concatenate([top, top, rest], axis=0)
         rows_j = block_rows(s, 1)
 
-        def sums(t, term_j, s=s, stacked=stacked, rows_j=rows_j):
-            spread = dot_fast(m.xt[s, pl.ds(pl.multiple_of(t * 512, 512), 512), :], stacked)
-            spread = spread.reshape(8, EDGE, RANK)
-            m.terms[pl.ds(pl.multiple_of(2 * EDGE * s + t * 8, 8), 8), :] = jnp.sum(
-                spread * rows_j[None], axis=1
-            )
-            return term_j + jnp.sum(spread * eight_rows(s, t)[:, None, :], axis=0)
+        m.spread[...] = dot_fast(m.xt[s], stacked)
+
+        def sums(t, term_j, s=s, rows_j=rows_j):
+            for k in range(8):
+                i = t * 8 + k
+                part = m.spread[pl.ds(pl.multiple_of(i * EDGE, EDGE), EDGE), :]
+                m.terms[pl.ds(2 * EDGE * s + i, 1), :] = jnp.sum(
+                    part * rows_j, axis=0, keepdims=True
+                )
+                term_j = term_j + part * m.picks[pl.ds(2 * EDGE * s + i, 1), :]
+            return term_j
 
         term_j = lax.fori_loop(0, 8, sums, jnp.zeros((EDGE, RANK), F32))
         m.terms[EDGE * (2 * s + 1) : EDGE * (2 * s + 2), :] = term_j
-        for xx in range(NX):
-            for side in range(2):
-                for h in range(HALVES):
-                    block = 2 * s + side
-                    m.orb[pl.ds(8 * NY * xx + 2 * block + h, NY, stride=8), :] = m.terms[
-                        pl.ds(EDGE * block + NW * h + xx, NY, stride=NX), :
-                    ]
+        for side in range(2):
+            for h in range(HALVES):
+                block = 2 * s + side
+                m.orb[pl.ds(2 * block + h, NW, stride=8), :] = m.terms[
+                    EDGE * block + NW * h : EDGE * block + NW * (h + 1), :
+                ]
         if s == 0:
             tile_core.wait_recv()
             m.tile_sum[...] = m.tile[...] + m.tile_core[...]
             tile_z = over_z("tile_sz", lambda peer: m.tile_sum, m.tile_z, 8)
             m.tile_z[pl.ds(pl.multiple_of(z * 8, 8), 8), :] = m.tile_sum[...]
-    size = 8 * NY
-    orb_x = over_x("orb_sx", lambda peer: rows_of(m.orb, peer, 8 * NY), m.orb_mid, size)
-    keep(m.orb_mid, x, size, m.orb, x)
+    to_all("orb_s", lambda peer: rows_of(m.orb, peer, 8), rows_of(m.orb_in, w, 8))
+    keep(m.orb_in, w, 8, m.orb, w)
 
     arrived(tile_z)
     total = m.tile_z[0:8, :]
@@ -530,12 +542,6 @@
     tile_y = over_y("tile_sy", lambda peer: m.tile_all, m.tile_y, 8)
     m.tile_y[pl.ds(pl.multiple_of(y * 8, 8), 8), :] = total
 
-    arrived(orb_x)
-    turn_around(m.orb_mid, m.orb_turn, 8)
-    size = 8 * NX
-    orb_y = over_y("orb_sy", lambda peer: rows_of(m.orb_turn, peer, 8 * NX), m.orb_in, size)
-    keep(m.orb_in, y, size, m.orb_turn, y)
-
     arrived(own_y)
     for yy in range(NY):
         aux_out[NX * yy : NX * yy + NX, :] = m.own_in[8 * yy : 8 * yy + NX, :]
@@ -545,7 +551,7 @@
     tile_x = over_x("tile_sx", lambda peer: m.tile_y, m.tile_x, size)
     m.tile_x[pl.ds(pl.multiple_of(x * size, 8), size), :] = m.tile_y[...]
 
-    arrived(orb_y)
+    all_in("orb_s", m.orb_in.at[pl.ds(0, 8 * (NW - 1))])
     m.dense[...] = dot_full(m.pick_orb[0 : 16 * nz, :], m.orb_in[...])
     size = 8 * nz
     dense_core = send(rows_of(m.dense, 1 - core, size), m.dense_core, "dense_sc", 0, narrow=partner)
@@ -584,6 +590,9 @@
                 ]
     for copy in pending:
         copy.wait_send()
+    all_in("fwd_s", m.fwd.at[pl.ds(0, NW - 1)], sent)
+    all_in("rep_s", m.rep.at[pl.ds(0, 8 * (NW - 1))], sent)
+    all_in("orb_s", m.orb.at[pl.ds(0, 8 * (NW - 1))], sent)
 
 
 def on_device(blocks, block_coords, block_count, orbital_factor, *, nz):
@@ -597,9 +606,9 @@
             jax.ShapeDtypeStruct((CHUNK, RANK), F32),
         ),
         in_specs=[
-            pl.BlockSpec(memory_space=pltpu.SMEM),
-            pl.BlockSpec(memory_space=pltpu.SMEM),
-            pl.BlockSpec(memory_space=pltpu.VMEM),
+            pl.BlockSpec(memory_space=pl.ANY),
+            pl.BlockSpec(memory_space=pl.ANY),
+            pl.BlockSpec(memory_space=pl.ANY),
             pl.BlockSpec(memory_space=pl.ANY),
         ],
         out_specs=(
@@ -608,7 +617,7 @@
         ),
         scratch_shapes=scratch,
         compiler_params=pltpu.CompilerParams(
-            collective_id=0, has_side_effects=True, vmem_limit_bytes=48 << 20
+            collective_id=0, has_side_effects=True, vmem_limit_bytes=67_043_328 - (160 << 10)
         ),
     )(
         block_coords.reshape(2, 3),

time: 90.7 us -> 82.5 us (0.910)
  the two profiles are of different devices: /device:TPU:1 before, /device:TPU:8 now
where the time goes in v2:
time: 82.5 us; the launch traced here: 82.3 us
  Pallas kernels  78.1 us (95%)
  local copies, waits for them, and re-layouts  2.89 us (4%)
  between operations  1.28 us (2%)
    pallas_call x1, Pallas kernels, on_device(): pl.pallas_call(functools.partial(kernel, nz), out_shape=(jax.ShapeDtypeSt...  78.1 us
    unnamed x2, local copies, waits for them, and re-layouts  2.89 us

profile of v2, /device:TPU:8, one launch (start us, length us, event | category | flops | bytes accessed | tf_op | source)
XLA Modules:
  0.0 82.3 jit_solution(13350766109862764305)
XLA Ops:
  1.3 78.1 %shard_map.59 = (f32[32,128]{1,0:T(8,128)}, f32[256,128]{1,0:T(8,128)}) custom-call(s32[2,3]{1,0:T(2,128)} %bitcast.5, s32[1,1]{1,0:T(1,128)S(6)} %copy.8.count, f32[256,128]{1,0:T(8,128)} %b_in.1, f32[2,64,4096]{2,1,0:T(8,128)} %bitcast.3), custom_call_target="tpu_custom_call" | custom-call | tf_op jit(solution)/shard_map/pallas_call | solution.py:602
  79.4 1.3 %copy.9 = f32[1,32,128]{2,1,0:T(8,128)} copy(f32[1,32,128]{2,1,0:T(8,128)} %bitcast.4) | data formatting | bytes 32768
  80.8 1.6 %copy.10 = f32[256,128]{1,0:T(8,128)} copy(f32[256,128]{1,0:T(8,128)} %get-tuple-element.9) | data formatting | bytes 262144

commit v3 on v2

--- a/solution.py
+++ b/solution.py
@@ -103,14 +103,16 @@
         pick_aux_t=((4 * NW, RANK), F32),
         pick_aux=((RANK, 4 * NW), F32),
         pick_orb_t=((8 * NW, RANK), F32),
-        pick_orb=((RANK, 8 * NW), F32),
-        pick_reply=((8 * NW, RANK), F32),
+        pick_orb=((2, RANK, 4 * NW), F32),
         terms=((4 * EDGE, RANK), F32),
         fwd=((NW, 4, RANK), F32),
         fwd_in=((NW, 4, RANK), F32),
         fwd_rows=((4 * NW, RANK), F32),
-        rep=((8 * NW, RANK), F32),
-        rep_in=((8 * NW, RANK), F32),
+        rep=((NW, 4, RANK), F32),
+        rep_in=((NW, 4, RANK), F32),
+        rep_rows=((4 * NW, RANK), F32),
+        tri=((NW, 4, RANK), F32),
+        tri_in=((NW, 4, RANK), F32),
         own=((NW, RANK), F32),
         own_mid=((NW, RANK), F32),
         own_turn=((8 * NY, RANK), F32),
@@ -123,8 +125,12 @@
         tile_z=((8 * nz, RANK), F32),
         tile_y=((8 * NY, RANK), F32),
         tile_x=((8 * NW, RANK), F32),
-        orb=((8 * NW, RANK), F32),
-        orb_in=((8 * NW, RANK), F32),
+        orb_0=((NW, 4, RANK), F32),
+        orb_1=((NW, 4, RANK), F32),
+        orb_in_0=((NW, 4, RANK), F32),
+        orb_in_1=((NW, 4, RANK), F32),
+        orb_rows=((4 * NW, RANK), F32),
+        got_rows=((4 * NW, RANK), F32),
         dense=((16 * nz, RANK), F32),
         dense_core=((8 * nz, RANK), F32),
         part=((8 * nz, RANK), F32),
@@ -143,13 +149,15 @@
         meta_sy=NY,
         fwd_s=1,
         rep_s=1,
+        tri_s=1,
         own_sx=NX,
         own_sy=NY,
         tile_sc=1,
         tile_sz=nz,
         tile_sy=NY,
         tile_sx=NX,
-        orb_s=1,
+        orb_0=1,
+        orb_1=1,
         dense_sc=1,
         part_sz=nz,
         sum_sy=NY,
@@ -222,6 +230,17 @@
                         device_id_type=pl.DeviceIdType.MESH,
                     ).start()
 
+    def send_pieces(name, rows, pieces, into):
+        for k in range(NW):
+            pieces[k] = rows[4 * k : 4 * k + 4, :]
+        to_all(name, lambda peer: pieces.at[peer], into.at[w])
+        into[w] = pieces[w]
+
+    def take_pieces(name, into, rows):
+        all_in(name, into.at[pl.ds(0, NW - 1)])
+        for k in range(NW):
+            rows[4 * k : 4 * k + 4, :] = into[k]
+
     def all_in(name, others, which=None):
         sem = (got if which is None else which)[name].at[0]
         pltpu.make_async_copy(others, others, sem).wait()
@@ -261,7 +280,7 @@
     pl.semaphore_signal(barrier, inc=1, device_id=(w, partner), device_id_type=pl.DeviceIdType.MESH)
 
     m.picks[...] = jnp.zeros_like(m.picks)
-    m.pick_reply[...] = jnp.zeros_like(m.pick_reply)
+    m.tile[...] = jnp.zeros_like(m.tile)
     m.meta_row[...] = jnp.zeros_like(m.meta_row)
 
     loads[1].wait()
@@ -414,13 +433,15 @@
             if t < 2:
                 hot = jnp.where(lanes == place + QB * h, 1.0, 0.0)
                 m.pick_aux_t[pl.ds(2 * t + h, NW, stride=4), :] = hot
-                m.pick_reply[pl.ds(2 * t + h, NW, stride=8), :] = hot
             else:
-                m.pick_orb_t[pl.ds(2 * (t - 2) + h, NW, stride=8), :] = jnp.where(
+                side = (t - 2) % 2
+                start = 4 * NW * ((t - 2) // 2) + 2 * side + h
+                m.pick_orb_t[pl.ds(start, NW, stride=4), :] = jnp.where(
                     lanes == place + 4 * h, 1.0, 0.0
                 )
     m.pick_aux[...] = m.pick_aux_t[...].T
-    m.pick_orb[...] = m.pick_orb_t[...].T
+    for s in range(2):
+        m.pick_orb[s] = m.pick_orb_t[4 * NW * s : 4 * NW * (s + 1), :].T
     pick_partner(half_way)
 
     def block_rows(s, side):
@@ -452,28 +473,21 @@
             m.fwd_rows[pl.ds(2 * s + h, NW, stride=4), :] = m.terms[
                 EDGE * s + NW * h : EDGE * s + NW * (h + 1), :
             ]
-    for k in range(NW):
-        m.fwd[k] = m.fwd_rows[4 * k : 4 * k + 4, :]
-    to_all("fwd_s", lambda peer: m.fwd.at[peer], m.fwd_in.at[w])
-    m.fwd_in[w] = m.fwd[w]
+    send_pieces("fwd_s", m.fwd_rows, m.fwd, m.fwd_in)
 
     grams.wait_recv()
     m.gram_b[...] = m.gram[...] + m.gram_in[...]
     m.inv[...] = m.gram_b[...] * m.gram_b[...]
     invert_steps(m.inv, 0, 16)
-    all_in("fwd_s", m.fwd_in.at[pl.ds(0, NW - 1)])
-    for k in range(NW):
-        m.fwd_rows[4 * k : 4 * k + 4, :] = m.fwd_in[k]
+    take_pieces("fwd_s", m.fwd_in, m.fwd_rows)
 
     aux_sum = dot_full(m.pick_aux[0 : HALVES * QB, :], m.fwd_rows[...])
     aux_own = dot_full(aux_sum, m.inv[...])
 
-    m.rep[...] = dot_full(m.pick_reply[:, 0 : HALVES * QB], aux_own)
+    m.rep_rows[...] = dot_full(m.pick_aux_t[:, 0 : HALVES * QB], aux_own)
+    send_pieces("rep_s", m.rep_rows, m.rep, m.rep_in)
     m.gram_own[...] = dot_full(aux_own.T, aux_own)
-    for k in range(NW):
-        m.rep[8 * k + 4 : 8 * k + 8, :] = m.gram_own[4 * k : 4 * k + 4, :]
-    to_all("rep_s", lambda peer: rows_of(m.rep, peer, 8), rows_of(m.rep_in, w, 8))
-    keep(m.rep_in, w, 8, m.rep, w)
+    send_pieces("tri_s", m.gram_own, m.tri, m.tri_in)
 
     to = lax.broadcasted_iota(jnp.int32, (NW, HALVES * QB), 0)
     what = lax.broadcasted_iota(jnp.int32, (NW, HALVES * QB), 1)
@@ -490,16 +504,11 @@
     own_y = over_y("own_sy", lambda peer: rows_of(m.own_turn, peer, 8), m.own_in, 8)
     keep(m.own_in, y, 8, m.own_turn, y)
 
-    all_in("rep_s", m.rep_in.at[pl.ds(0, 8 * (NW - 1))])
-    total = m.rep_in[0:8, :]
-    for k in range(1, NW):
-        total = total + m.rep_in[8 * k : 8 * k + 8, :]
-    m.tile[...] = total
-    tile_core = send(m.tile, m.tile_core, "tile_sc", 0, narrow=partner)
+    take_pieces("rep_s", m.rep_in, m.rep_rows)
 
     for s in range(2):
         aux_rows = jnp.concatenate(
-            [m.rep_in[pl.ds(2 * s + h, NW, stride=8), :] for h in range(HALVES)], axis=0
+            [m.rep_rows[pl.ds(2 * s + h, NW, stride=4), :] for h in range(HALVES)], axis=0
         )
         top = aux_rows.astype(BF16)
         rest = (aux_rows - top.astype(F32)).astype(BF16)
@@ -522,17 +531,26 @@
         m.terms[EDGE * (2 * s + 1) : EDGE * (2 * s + 2), :] = term_j
         for side in range(2):
             for h in range(HALVES):
-                block = 2 * s + side
-                m.orb[pl.ds(2 * block + h, NW, stride=8), :] = m.terms[
-                    EDGE * block + NW * h : EDGE * block + NW * (h + 1), :
-                ]
+                start = EDGE * (2 * s + side) + NW * h
+                m.orb_rows[pl.ds(2 * side + h, NW, stride=4), :] = m.terms[start : start + NW, :]
         if s == 0:
-            tile_core.wait_recv()
-            m.tile_sum[...] = m.tile[...] + m.tile_core[...]
-            tile_z = over_z("tile_sz", lambda peer: m.tile_sum, m.tile_z, 8)
-            m.tile_z[pl.ds(pl.multiple_of(z * 8, 8), 8), :] = m.tile_sum[...]
-    to_all("orb_s", lambda peer: rows_of(m.orb, peer, 8), rows_of(m.orb_in, w, 8))
-    keep(m.orb_in, w, 8, m.orb, w)
+            send_pieces("orb_0", m.orb_rows, m.orb_0, m.orb_in_0)
+            all_in("tri_s", m.tri_in.at[pl.ds(0, NW - 1)])
+            total = m.tri_in[0]
+            for k in range(1, NW):
+                total = total + m.tri_in[k]
+            m.tile[4:8, :] = total
+            tile_core = send(m.tile, m.tile_core, "tile_sc", 0, narrow=partner)
+        else:
+            send_pieces("orb_1", m.orb_rows, m.orb_1, m.orb_in_1)
+    tile_core.wait_recv()
+    m.tile_sum[...] = m.tile[...] + m.tile_core[...]
+    tile_z = over_z("tile_sz", lambda peer: m.tile_sum, m.tile_z, 8)
+    m.tile_z[pl.ds(pl.multiple_of(z * 8, 8), 8), :] = m.tile_sum[...]
+
+    arrived(own_y)
+    for yy in range(NY):
+        aux_out[NX * yy : NX * yy + NX, :] = m.own_in[8 * yy : 8 * yy + NX, :]
 
     arrived(tile_z)
     total = m.tile_z[0:8, :]
@@ -542,23 +560,29 @@
     tile_y = over_y("tile_sy", lambda peer: m.tile_all, m.tile_y, 8)
     m.tile_y[pl.ds(pl.multiple_of(y * 8, 8), 8), :] = total
 
-    arrived(own_y)
-    for yy in range(NY):
-        aux_out[NX * yy : NX * yy + NX, :] = m.own_in[8 * yy : 8 * yy + NX, :]
-
-    arrived(tile_y)
-    size = 8 * NY
-    tile_x = over_x("tile_sx", lambda peer: m.tile_y, m.tile_x, size)
-    m.tile_x[pl.ds(pl.multiple_of(x * size, 8), size), :] = m.tile_y[...]
-
-    all_in("orb_s", m.orb_in.at[pl.ds(0, 8 * (NW - 1))])
-    m.dense[...] = dot_full(m.pick_orb[0 : 16 * nz, :], m.orb_in[...])
+    take_pieces("orb_0", m.orb_in_0, m.got_rows)
+    m.dense[...] = dot_full(m.pick_orb[0, 0 : 16 * nz, :], m.got_rows[...])
+    take_pieces("orb_1", m.orb_in_1, m.got_rows)
+    m.dense[...] = m.dense[...] + dot_full(m.pick_orb[1, 0 : 16 * nz, :], m.got_rows[...])
     size = 8 * nz
     dense_core = send(rows_of(m.dense, 1 - core, size), m.dense_core, "dense_sc", 0, narrow=partner)
     dense_core.wait_recv()
     m.part[...] = m.dense[pl.ds(pl.multiple_of(core * size, 8), size), :] + m.dense_core[...]
     part_z = over_z("part_sz", lambda peer: rows_of(m.part, peer, 8), m.part_z, 8)
     keep(m.part_z, z, 8, m.part, z)
+
+    arrived(tile_y)
+    size = 8 * NY
+    tile_x = over_x("tile_sx", lambda peer: m.tile_y, m.tile_x, size)
+    m.tile_x[pl.ds(pl.multiple_of(x * size, 8), size), :] = m.tile_y[...]
+
+    arrived(part_z)
+    total = m.part_z[0:8, :]
+    for k in range(1, nz):
+        total = total + m.part_z[8 * k : 8 * k + 8, :]
+    m.sum_own[...] = total
+    sum_y = over_y("sum_sy", lambda peer: m.sum_own, m.sum_y, 8)
+    m.sum_y[pl.ds(pl.multiple_of(y * 8, 8), 8), :] = total
 
     arrived(tile_x)
     for xx in range(NX):
@@ -567,19 +591,11 @@
             m.gram_a[to_row : to_row + 4, :] = m.tile_x[at : at + 4, :]
     m.inv[...] = 2.0 * m.gram_a[...] * m.gram_b[...]
     invert_steps(m.inv, 0, 8)
-
-    arrived(part_z)
-    total = m.part_z[0:8, :]
-    for k in range(1, nz):
-        total = total + m.part_z[8 * k : 8 * k + 8, :]
-    m.sum_own[...] = total
-    sum_y = over_y("sum_sy", lambda peer: m.sum_own, m.sum_y, 8)
-    m.sum_y[pl.ds(pl.multiple_of(y * 8, 8), 8), :] = total
-    invert_steps(m.inv, 8, 16)
     arrived(sum_y)
     size = 8 * NY
     sum_x = over_x("sum_sx", lambda peer: m.sum_y, m.sum_x, size)
     m.sum_x[pl.ds(pl.multiple_of(x * size, 8), size), :] = m.sum_y[...]
+    invert_steps(m.inv, 8, 16)
     arrived(sum_x)
     m.final[...] = dot_full(m.sum_x[...], m.inv[...])
     for xx in range(NX):
@@ -590,9 +606,14 @@
                 ]
     for copy in pending:
         copy.wait_send()
-    all_in("fwd_s", m.fwd.at[pl.ds(0, NW - 1)], sent)
-    all_in("rep_s", m.rep.at[pl.ds(0, 8 * (NW - 1))], sent)
-    all_in("orb_s", m.orb.at[pl.ds(0, 8 * (NW - 1))], sent)
+    for name, pieces in (
+        ("fwd_s", m.fwd),
+        ("rep_s", m.rep),
+        ("tri_s", m.tri),
+        ("orb_0", m.orb_0),
+        ("orb_1", m.orb_1),
+    ):
+        all_in(name, pieces.at[pl.ds(0, NW - 1)], sent)
 
 
 def on_device(blocks, block_coords, block_count, orbital_factor, *, nz):

time: 82.5 us -> 79.1 us (0.959)
  the two profiles are of different devices: /device:TPU:8 before, /device:TPU:1 now
where the time goes in v3:
time: 79.1 us; the launch traced here: 78.6 us
  Pallas kernels  74.4 us (94%)
  local copies, waits for them, and re-layouts  2.89 us (4%)
  between operations  1.28 us (2%)
    pallas_call x1, Pallas kernels, on_device(): pl.pallas_call(functools.partial(kernel, nz), out_shape=(jax.ShapeDtypeSt...  74.4 us
    unnamed x2, local copies, waits for them, and re-layouts  2.89 us

profile of v3, /device:TPU:1, one launch (start us, length us, event | category | flops | bytes accessed | tf_op | source)
XLA Modules:
  0.0 78.6 jit_solution(9090375552143569348)
XLA Ops:
  1.3 74.4 %shard_map.59 = (f32[32,128]{1,0:T(8,128)}, f32[256,128]{1,0:T(8,128)}) custom-call(s32[2,3]{1,0:T(2,128)} %bitcast.5, s32[1,1]{1,0:T(1,128)S(6)} %copy.8.count, f32[256,128]{1,0:T(8,128)} %b_in.1, f32[2,64,4096]{2,1,0:T(8,128)} %bitcast.3), custom_call_target="tpu_custom_call" | custom-call | tf_op jit(solution)/shard_map/pallas_call | solution.py:623
  75.7 1.3 %copy.9 = f32[1,32,128]{2,1,0:T(8,128)} copy(f32[1,32,128]{2,1,0:T(8,128)} %bitcast.4) | data formatting | bytes 32768
  77.0 1.6 %copy.10 = f32[256,128]{1,0:T(8,128)} copy(f32[256,128]{1,0:T(8,128)} %get-tuple-element.9) | data formatting | bytes 262144

commit v4 on v3

--- a/solution.py
+++ b/solution.py
@@ -16,7 +16,8 @@
 QB = 16
 SPAN = EDGE * EDGE
 CHUNK = 256
-SUB = CHUNK // 2
+PARTS = 4
+SUB = CHUNK // PARTS
 F32, BF16 = jnp.float32, jnp.bfloat16
 HIGHEST = lax.Precision.HIGHEST
 
@@ -141,9 +142,9 @@
     )
     sems = dict(
         load=4,
-        up=8,
-        down=8,
-        across=16,
+        up=PARTS * nz // 2,
+        down=PARTS * nz // 2,
+        across=PARTS * nz,
         grams=1,
         meta_sx=NX,
         meta_sy=NY,
@@ -349,7 +350,7 @@
             src,
             piece_at(step, part, back),
             "down" if back else "up",
-            2 * step + part,
+            PARTS * step + part,
             narrow=peer * 2 + core,
         )
 
@@ -363,17 +364,17 @@
 
     def parts_of(step, back):
         if step < half_way:
-            return (0, 1)
-        return (1,) if back else (0,)
+            return range(PARTS)
+        return range(PARTS // 2, PARTS) if back else range(PARTS // 2)
 
     hops = {}
-    for part in (0, 1):
+    for part in range(PARTS):
         for back in (False, True):
             if part in parts_of(1, back):
                 hops[1, part, back] = hop(0, part, back)
     meta_x = over_x("meta_sx", lambda peer: m.meta, m.meta_x, 8)
     m.meta_x[pl.ds(pl.multiple_of(x * 8, 8), 8), :] = m.meta[...]
-    for part in (0, 1):
+    for part in range(PARTS):
         to_partner(0, part, False)
     pick_chunk(c)
     own_chunk = m.mine[...]
@@ -390,7 +391,8 @@
         m.gram[...] += dot_full(chunk.T, chunk)
 
     def pick_partner(step):
-        first, last = (0, 2) if step == 0 else (4 * step - 2, min(4 * step + 2, 4 * half_way))
+        first = 0 if step == 0 else PARTS * (2 * step - 1)
+        last = min(PARTS * (2 * step + 1), PARTS * nz)
         arrived(across[first:last])
         pick_chunk((z + step) % nz * 2 + 1 - core)
         if 0 < step < half_way:
@@ -398,7 +400,7 @@
 
     meta_y = None
     for step in range(1, half_way + 1):
-        for part in (0, 1):
+        for part in range(PARTS):
             for back in (False, True):
                 if part not in parts_of(step, back):
                     continue
@@ -638,7 +640,7 @@
         ),
         scratch_shapes=scratch,
         compiler_params=pltpu.CompilerParams(
-            collective_id=0, has_side_effects=True, vmem_limit_bytes=67_043_328 - (160 << 10)
+            collective_id=0, has_side_effects=True, vmem_limit_bytes=(54 << 20) - (240 << 10)
         ),
     )(
         block_coords.reshape(2, 3),

time: 79.1 us -> 76.9 us (0.972)
  Pallas kernels: 74.4 us -> 73.2 us
  local copies, waits for them, and re-layouts: 2.89 us -> 1.93 us
    pallas_call x1, Pallas kernels: 74.4 us -> 73.2 us  [on_device(): pl.pallas_call(functools.partial(kernel, nz), out_shape=(jax.ShapeDtypeSt...]
    unnamed x2 -> x4, local copies, waits for them, and re-layouts: 2.89 us -> 1.93 us
where the time goes in v4:
time: 76.9 us; the launch traced here: 76.4 us
  Pallas kernels  73.2 us (95%)
  local copies, waits for them, and re-layouts  1.93 us (3%)
  between operations  1.29 us (2%)
    pallas_call x1, Pallas kernels, on_device(): pl.pallas_call(functools.partial(kernel, nz), out_shape=(jax.ShapeDtypeSt...  73.2 us
    unnamed x4, local copies, waits for them, and re-layouts  1.93 us

profile of v4, /device:TPU:1, one launch (start us, length us, event | category | flops | bytes accessed | tf_op | source)
XLA Modules:
  0.0 76.4 jit_solution(66525200963897962)
XLA Ops:
  1.3 0.0 copy-start
  1.3 0.7 copy-done
  2.0 73.2 %shard_map.59 = (f32[32,128]{1,0:T(8,128)S(1)}, f32[256,128]{1,0:T(8,128)S(1)}) custom-call(s32[2,3]{1,0:T(2,128)S(1)} %bitcast.4, s32[1,1]{1,0:T(1,128)S(6)} %copy.8.count, f32[256,128]{1,0:T(8,128)} %b_in.1, f32[2,64,4096]{2,1,0:T(8,128)} %bitcast.5), custom_call_target="tpu_custom_call" | custom-call | tf_op jit(solution)/shard_map/pallas_call | solution.py:625
  75.2 0.6 copy.9
  75.8 0.7 copy.10
Async XLA Ops:
  1.3 0.7 copy-start
